TPU v7x, 128 devices: a whole 4x4x4 slice. The times are simulated.
128 devices in a mesh: region: 8 (over x, core), tile: 16 (over z, y).
Axes of the slice: x: 4, y: 4, z: 4, core: 2. Of those that a mesh axis runs over, the one named last changes fastest.
Arguments:
- coefficients: bfloat16 [131072, 145], P(('region', 'tile')), may hold values from 0.0009994507 to 0.019897461
- peak_power: bfloat16 [131072], P(('region', 'tile')), may hold values from 0.5 to 4
- inverter_limit: bfloat16 [131072], P(('region', 'tile')), may hold values from 0.5 to 3
- building_feeder: int32 [131072, 1], P(('region', 'tile')), may hold values from 0 to 127; in each aligned block of 1024 rows (0 to 1023, 1024 to 2047, ...) at most 16 rows name the same one
- building_node: int32 [131072], P(('region', 'tile')), may hold values from 0 to 2047
- sky_radiance: bfloat16 [145, 768], replicated, may hold values from 0.0099487305 to 10
- feeder_nodes: int32 [128], P(('region', 'tile')), may hold values from 1 to 2048, 163840 in all
- sensitivity: bfloat16 [128, 2048, 2048], P(('region', 'tile')), may hold values from -0.125 to 0.125
- feeder_substation: int32 [128], P(('region', 'tile')), may hold values from 0 to 31
- mv_sensitivity: float32 [32, 32], replicated, may hold values from -1 to 1
Outputs:
- node_voltage: bfloat16 [128, 2048, 768], P(('region', 'tile'))
Inputs may be any that keep to these rules, and one draw needn't show every extreme that they name: `building_feeder`: among the rows of one device no feeder is named more than 16 times, a bound that some block reaches. `feeder_nodes`: the counts sum to 128 * 2048 * 5 // 8 and the largest is exactly 2048.
All inputs are finite; a program needn't handle non-finite values. No bound on the sum of `feeder_nodes` on one device may be relied on, other than what follows from the above.
Results may differ from a plain program's by a relative error of at most 0.0006.
The roundings to bfloat16 on the way count: a program that leaves them out, or rounds other values in their place, can miss the bound.
Values may be sent and summed in bfloat16 or wider, within the bound.
A program may use at most 64 MiB of HBM per device.

v0:
```python
import jax
import jax.numpy as jnp
from jax import lax
from jax.sharding import PartitionSpec as P


def solar_power(coef_rows, peak_rows, limit_rows, sky_table):
    raw_power = jnp.dot(coef_rows, sky_table, preferred_element_type=jnp.float32)
    scaled = raw_power * peak_rows.astype(jnp.float32)[:, None]
    return jnp.minimum(scaled, limit_rows.astype(jnp.float32)[:, None]).astype(jnp.bfloat16)


def move_rows(main_rows, node_buffer):
    got_main, got_nodes = (
        lax.all_to_all(main_rows, ("region", "tile"), split_axis=0, concat_axis=0, tiled=True),
        lax.all_to_all(node_buffer, ("region", "tile"), split_axis=0, concat_axis=0, tiled=True),
    )
    return (got_main, got_nodes)


def on_device(
    coefficients,
    peak_power,
    inverter_limit,
    building_feeder,
    building_node,
    sky_radiance,
    feeder_nodes,
    sensitivity,
    feeder_substation,
    mv_sensitivity,
):
    per_device = coefficients.shape[0]
    regions = lax.axis_size("region")
    tiles = lax.axis_size("tile")
    feeders = regions * tiles
    capacity = 2 * per_device // feeders
    slot_count = feeders * capacity
    node_slots = sensitivity.shape[1]
    columns = sky_radiance.shape[1]
    target = building_feeder[:, 0]
    matches = (target[:, None] == jnp.arange(feeders, dtype=jnp.int32)[None, :]).astype(jnp.int32)
    earlier = jnp.cumsum(matches, axis=0) - matches
    position = target * capacity + jnp.sum(earlier * matches, axis=1)
    node_buffer = jnp.full((slot_count,), -1, jnp.int32).at[position].set(building_node)
    pv_rows = solar_power(coefficients, peak_power, inverter_limit, sky_radiance)
    pv_buffer = jnp.zeros((slot_count, columns), jnp.bfloat16).at[position].set(pv_rows)
    got_power, got_nodes = move_rows(pv_buffer, node_buffer)
    live_count = feeder_nodes[0]
    valid = got_nodes >= 0
    local_node = jnp.where(valid, got_nodes % live_count, node_slots)
    inject = (
        jnp.zeros((node_slots, columns), jnp.float32)
        .at[local_node]
        .add(got_power.astype(jnp.float32), mode="drop")
    )
    head_flow = jnp.sum(inject, axis=0) / (4.0 * per_device)
    substations = mv_sensitivity.shape[0]
    own_station = feeder_substation[0]
    station_match = jnp.arange(substations, dtype=jnp.int32)[:, None] == own_station
    contribution = jnp.where(station_match, head_flow[None, :], 0.0)
    totals = lax.psum(contribution, ("region", "tile"))
    medium = jnp.dot(mv_sensitivity, totals, precision=lax.Precision.HIGHEST)
    base_volt = jnp.sum(jnp.where(station_match, medium, 0.0), axis=0)
    rise = jnp.dot(sensitivity[0], inject.astype(jnp.bfloat16), preferred_element_type=jnp.float32)
    live = jnp.arange(node_slots, dtype=jnp.int32) < live_count
    voltage = jnp.where(live[:, None], base_volt[None, :] + rise, 0.0).astype(jnp.bfloat16)
    return voltage[None, :, :]


def solution(mesh):
    return jax.shard_map(
        on_device,
        mesh=mesh,
        in_specs=(
            P(("region", "tile"), None),
            P(("region", "tile")),
            P(("region", "tile")),
            P(("region", "tile"), None),
            P(("region", "tile")),
            P(),
            P(("region", "tile")),
            P(("region", "tile"), None, None),
            P(("region", "tile")),
            P(),
        ),
        out_specs=P(("region", "tile"), None, None),
        check_vma=False,
    )
```

profile of v0, /device:TPU:1, one launch (start us, length us, event | category | flops | bytes accessed | tf_op | source)
XLA Modules:
  0.0 264.5 jit_solution(1899995458058566772)
XLA Ops:
  6.5 0.0 copy-start
  6.5 0.0 copy-start.1
  6.5 0.0 copy-start.3
  6.5 0.0 copy-start.5
  6.5 0.0 copy-start.4
  6.5 0.8 copy.20
  7.4 0.2 fusion.18
  7.7 0.1 copy.21
  7.8 1.0 fusion.17
  8.9 0.0 copy-done.1
  8.9 4.5 %scatter_custom_fusion = s32[2048]{0:T(1024)S(1)} fusion(s32[1024]{0:T(1024)S(1)} %bitcast.45, s32[1024]{0:T(1024)} %param.14, s32[]{:T(128)} %constant.9.clone.1), kind=kCustom, calls=%fused_computation.34 | custom fusion | bytes 8704 | tf_op jit(solution)/shard_map/scatter | solution.py:45
  13.4 0.7 all_to_all.12
  14.1 11.5 %all-to-all-start = ((s32[128,16,1]{1,2,0:T(1,128)}), s32[128,16,1]{1,2,0:T(1,128)S(1)}, u32[]{:S(2)}, u32[]{:S(2)}) async-start(s32[128,16,1]{1,2,0:T(1,128)} %bitcast.9), calls=%async_computation | async-start | bytes 131072 | tf_op jit(solution)/shard_map/all_to_all | solution.py:16
  25.6 0.0 copy-done.3
  25.6 0.0 copy-done
  25.6 0.0 copy-done.5
  25.6 0.0 copy-done.4
  25.6 0.7 minimum_convert_fusion
  26.3 7.3 %scatter_custom_fusion.1 = bf16[2048,768]{1,0:T(8,128)(2,1)} fusion(s32[1024]{0:T(1024)S(1)} %bitcast.46, bf16[1024,768]{1,0:T(8,128)(2,1)S(1)} %minimum_convert_fusion, bf16[]{:T(256)} %constant.14.clone.1), kind=kCustom, calls=%fused_computation.12 | custom fusion | bytes 3145730 | tf_op jit(solution)/shard_map/scatter | solution.py:47
  33.6 1.8 all-to-all-done
  35.4 8.0 %all-to-all-start.1 = ((bf16[128,16,768]{2,1,0:T(8,128)(2,1)}), bf16[128,16,768]{2,1,0:T(8,128)(2,1)S(1)}, u32[]{:S(2)}, u32[]{:S(2)}) async-start(bf16[128,16,768]{2,1,0:T(8,128)(2,1)} %bitcast.11), calls=%async_computation.1 | async-start | bytes 6291456 | tf_op jit(solution)/shard_map/all_to_all | solution.py:15
  43.4 0.2 all-reduce.2.cloned.1.call-start
  44.9 5.7 %remainder_reduce_fusion = s32[128,16]{1,0:T(8,128)} fusion(s32[128,16,1]{1,2,0:T(1,128)S(1)} %all-to-all-done, s32[]{:T(128)S(6)} %select_n.57), kind=kLoop, calls=%fused_computation.26 | loop fusion | flops 2048 | bytes 16388 | tf_op jit(solution)/shard_map/jit(remainder)/rem | solution.py:51
  50.6 0.9 rem.22
  51.5 0.2 compare_reduce_fusion
  51.7 0.1 ge.14
  51.9 31.7 %all-to-all-done.1 = bf16[128,16,768]{2,1,0:T(8,128)(2,1)S(1)} async-done(((bf16[128,16,768]{2,1,0:T(8,128)(2,1)}), bf16[128,16,768]{2,1,0:T(8,128)(2,1)S(1)}, u32[]{:S(2)}, u32[]{:S(2)}) %all-to-all-start.1) | async-done | bytes 3145760 | tf_op jit(solution)/shard_map/all_to_all | solution.py:15
  83.6 17.1 %scatter_custom_fusion.2 = f32[2048,768]{1,0:T(8,128)} fusion(s32[2048]{0:T(1024)S(1)} %bitcast.44, bf16[2048,768]{1,0:T(8,128)(2,1)S(1)} %bitcast.40, f32[]{:T(128)} %constant.8.clone.1), kind=kCustom, calls=%fused_computation.5 | custom fusion | flops 3145728 | bytes 9437188 | tf_op jit(solution)/shard_map/scatter-add | solution.py:55
  100.6 0.0 copy-start.2
  100.6 3.2 %reduce_sum.31 = f32[768]{0:T(1024)S(1)} reduce(f32[2048,768]{1,0:T(8,128)} %scatter_custom_fusion.2, f32[]{:T(128)} %constant.8.clone.1), dimensions={0}, to_apply=%region_6.7 | reduce | flops 1572096 | bytes 6294532 | tf_op jit(solution)/shard_map/reduce_sum | solution.py:57
  103.9 0.7 broadcast_select_fusion
  104.6 0.0 all-reduce.2.cloned.1.call-update
  104.6 137.5 %all-reduce.2.cloned.1.call-done = f32[32,768]{1,0:T(8,128)} async-done(((f32[32,768]{1,0:T(8,128)}), f32[32,768]{1,0:T(8,128)}) %all-reduce.2.cloned.1.call-update) | async-done | bytes 98320 | tf_op jit(solution)/shard_map/psum | solution.py:62
  242.1 0.0 copy-done.2
  242.1 1.1 fusion.15
  243.2 11.7 %fusion.8 = bf16[1,2048,768]{1,2,0:T(8,128)(2,1)S(1)} fusion(bf16[1,2048,2048]{2,1,0:T(8,128)(2,1)} %param.17, f32[2048,768]{1,0:T(8,128)} %scatter_custom_fusion.2, f32[768]{0:T(1024)S(1)} %fusion.15, pred[2048]{0:T(1024)(128)(4,1)S(1)} %iota_compare_fusion.3), kind=kOutput, calls=%fused_computation.11 | convolution fusion | flops 6448742400 | bytes 17830912 | tf_op jit(solution)/shard_map/dot_general | solution.py:65
  254.9 2.8 %copy.23 = bf16[1,2048,768]{2,1,0:T(8,128)(2,1)} copy(bf16[1,2048,768]{1,2,0:T(8,128)(2,1)S(1)} %fusion.8) | data formatting | bytes 6291456 | tf_op jit(solution)/shard_map/broadcast_in_dim | solution.py:68
  (10 shorter events, 0.1 us)
Async XLA Ops:
  6.5 19.1 %copy-start = (bf16[1024,145]{0,1:T(8,128)(2,1)S(1)}, bf16[1024,145]{0,1:T(8,128)(2,1)}, u32[]{:S(2)}) copy-start(bf16[1024,145]{0,1:T(8,128)(2,1)} %param.10) | copy-start | bytes 890884
  6.5 2.3 copy-start.1
  6.5 19.0 %copy-start.3 = (bf16[1024]{0:T(1024)(128)(2,1)S(1)}, bf16[1024]{0:T(1024)(128)(2,1)}, u32[]{:S(2)}) copy-start(bf16[1024]{0:T(1024)(128)(2,1)} %param.11) | copy-start | bytes 6148
  6.5 19.1 %copy-start.5 = (bf16[1024]{0:T(1024)(128)(2,1)S(1)}, bf16[1024]{0:T(1024)(128)(2,1)}, u32[]{:S(2)}) copy-start(bf16[1024]{0:T(1024)(128)(2,1)} %param.12) | copy-start | bytes 6148
  6.5 19.1 %copy-start.4 = (bf16[145,768]{1,0:T(8,128)(2,1)S(1)}, bf16[145,768]{1,0:T(8,128)(2,1)}, u32[]{:S(2)}) copy-start(bf16[145,768]{1,0:T(8,128)(2,1)} %param.15) | copy-start | bytes 668164
  14.1 21.3 %all-to-all-start = ((s32[128,16,1]{1,2,0:T(1,128)}), s32[128,16,1]{1,2,0:T(1,128)S(1)}, u32[]{:S(2)}, u32[]{:S(2)}) async-start(s32[128,16,1]{1,2,0:T(1,128)} %bitcast.9), calls=%async_computation | async-start | bytes 131072 | tf_op jit(solution)/shard_map/all_to_all | solution.py:16
  35.4 48.2 %all-to-all-start.1 = ((bf16[128,16,768]{2,1,0:T(8,128)(2,1)}), bf16[128,16,768]{2,1,0:T(8,128)(2,1)S(1)}, u32[]{:S(2)}, u32[]{:S(2)}) async-start(bf16[128,16,768]{2,1,0:T(8,128)(2,1)} %bitcast.11), calls=%async_computation.1 | async-start | bytes 6291456 | tf_op jit(solution)/shard_map/all_to_all | solution.py:15
  43.4 198.7 %all-reduce.2.cloned.1.call-start = ((), (), s32[]{:S(2)}) async-start(), calls=%async_computation.2 | async-start | bytes 196608 | tf_op jit(solution)/shard_map/psum | solution.py:62
  100.6 141.4 %copy-start.2 = (f32[32,32]{1,0:T(8,128)S(1)}, f32[32,32]{1,0:T(8,128)}, u32[]{:S(2)}) copy-start(f32[32,32]{1,0:T(8,128)} %param.19) | copy-start | bytes 12292
Sparse Core Ops, SparseCore 0:
  104.7 137.2 all-reduce.1
where the time goes:
time: 265 us
  waiting for transfers between devices  171 us (65%)
  other arithmetic  28.3 us (11%)
  starting transfers between devices  19.7 us (7%)
  local copies, waits for them, and re-layouts  17.3 us (7%)
  between operations  14.9 us (6%)
  matrix products  13.5 us (5%)
    psum x1, waiting for transfers between devices, on_device(): totals = lax.psum(contribution, ('region', 'tile'))  137 us
    all_to_all x1, waiting for transfers between devices, move_rows(): lax.all_to_all(main_rows, ('region', 'tile'), split_axis=0, concat_axis=0...  31.7 us
    scatter-add x1, other arithmetic, on_device(): inject = jnp.zeros((node_slots, columns), jnp.float32).at[local_node].add...  17.1 us
    dot_general x1, matrix products, on_device(): jnp.dot(sensitivity[0], inject.astype(jnp.bfloat16), preferred_element_ty...  11.7 us
    all_to_all x1, starting transfers between devices, move_rows(): lax.all_to_all(node_buffer, ('region', 'tile'), split_axis=0, concat_axis...  11.5 us
    all_to_all x1, starting transfers between devices, move_rows(): lax.all_to_all(main_rows, ('region', 'tile'), split_axis=0, concat_axis=0...  7.98 us
    scatter x1, local copies, waits for them, and re-layouts, on_device(): jnp.zeros((slot_count, columns), jnp.bfloat16).at[position].set(pv_rows)  7.32 us
    rem x1, other arithmetic, on_device(): local_node = jnp.where(valid, got_nodes % live_count, node_slots)  5.66 us
  transfers between devices with their start and end apart: 3, of which 3 were waited for; matrix products, arithmetic and copies ran while one was open for 6% of the time, Pallas kernels for 0%

commit v1 on v0

v1 whole, which is shorter than its diff:
```python
import functools

import jax
import jax.numpy as jnp
from jax import lax
from jax.experimental import pallas as pl
from jax.experimental.pallas import tpu as pltpu
from jax.sharding import PartitionSpec as P

MESH = pl.DeviceIdType.MESH
F32 = jnp.float32
BF16 = jnp.bfloat16
I32 = jnp.int32

CAP = 16
WIDE = 256


def nt_dot(a, b):
    return lax.dot_general(a, b, (((1,), (1,)), ((), ())), preferred_element_type=F32)


def iota(shape, axis):
    return lax.broadcasted_iota(I32, shape, axis)


def exchange_kernel(
    regions,
    tiles,
    coef_ref,
    target_ref,
    node_ref,
    peak_ref,
    limit_ref,
    sky_ref,
    live_ref,
    station_ref,
    mv_ref,
    inject_ref,
    base_ref,
    features,
    sky_wide,
    send,
    recv,
    power,
    node_row,
    head,
    heads,
    send_sem,
    recv_sem,
    head_send_sem,
    head_recv_sem,
):
    feeders = regions * tiles
    patches, rows = coef_ref.shape
    columns = sky_ref.shape[1]
    nodes = inject_ref.shape[0]
    slots = feeders * CAP
    my_region, my_tile = lax.axis_index("region"), lax.axis_index("tile")
    me = my_region * tiles + my_tile

    def partner(step):
        region = lax.rem(my_region + step // tiles, regions)
        tile = lax.rem(my_tile + lax.rem(step, tiles), tiles)
        return region, tile

    barrier = pltpu.get_barrier_semaphore()

    def greet(step, carry):
        pl.semaphore_signal(barrier, inc=1, device_id=partner(step), device_id_type=MESH)
        return carry

    lax.fori_loop(1, feeders, greet, 0)

    target = target_ref[...]
    matches = jnp.where(iota((feeders, rows), 0) == target, 1.0, 0.0).astype(F32)
    blocks = rows // 128
    stacked = jnp.concatenate([matches[:, 128 * i : 128 * (i + 1)] for i in range(blocks)], axis=0).astype(BF16)
    left = iota((128, 256), 0) < iota((128, 256), 1)
    counter = jnp.where(left, 1.0, 0.0).astype(BF16)
    counts = jnp.dot(stacked, counter, preferred_element_type=F32)
    carry = jnp.zeros((feeders, 128), F32)
    ranks = []
    for i in range(blocks):
        part = counts[feeders * i : feeders * (i + 1)]
        mine = matches[:, 128 * i : 128 * (i + 1)]
        ranks.append(jnp.sum(mine * (part[:, :128] + carry), axis=0, keepdims=True))
        carry = carry + part[:, 128:]
    rank = jnp.concatenate(ranks, axis=1).astype(I32)
    position = target * CAP + rank

    aligned = patches // 16 * 16
    features[0:aligned, :] = coef_ref[0:aligned, :]
    tail = iota((16, rows), 0)
    raw_node = node_ref[...]
    digits = raw_node // 16
    last = coef_ref[aligned:patches, :].astype(F32)
    extra = jnp.where(tail == 0, jnp.broadcast_to(last, (16, rows)), 0.0)
    extra = jnp.where(tail == 1, peak_ref[...].astype(F32), extra)
    extra = jnp.where(tail == 2, limit_ref[...].astype(F32), extra)
    extra = jnp.where(tail == 3, digits.astype(F32), extra)
    extra = jnp.where(tail == 4, (raw_node - 16 * digits).astype(F32), extra)
    features[aligned : aligned + 16, :] = extra.astype(BF16)
    features[aligned + 16 :, :] = jnp.zeros((WIDE - aligned - 16, rows), BF16)
    sky_wide[0:aligned, :] = sky_ref[0:aligned, :]
    last_sky = jnp.broadcast_to(sky_ref[aligned:patches, :].astype(F32), (16, columns))
    sky_wide[aligned : aligned + 16, :] = jnp.where(iota((16, columns), 0) == 0, last_sky, 0.0).astype(BF16)
    sky_wide[aligned + 16 :, :] = jnp.zeros((WIDE - aligned - 16, columns), BF16)

    chunk = 256
    for i in range(slots // chunk):
        choose = jnp.where(iota((chunk, rows), 0) + chunk * i == position, 1.0, 0.0).astype(BF16)
        packed = nt_dot(choose, features[...]).astype(BF16)
        send[i * (chunk // CAP) : (i + 1) * (chunk // CAP)] = packed.reshape(chunk // CAP, CAP, WIDE)

    pl.semaphore_wait(barrier, feeders - 1)

    own = pltpu.make_async_copy(send.at[me], recv.at[me], recv_sem)
    own.start()

    def ship(step, carry):
        region, tile = partner(step)
        pltpu.make_async_remote_copy(
            src_ref=send.at[region * tiles + tile],
            dst_ref=recv.at[me],
            send_sem=send_sem,
            recv_sem=recv_sem,
            device_id=(region, tile),
            device_id_type=MESH,
        ).start()
        return carry

    lax.fori_loop(1, feeders, ship, 0)
    pltpu.make_async_copy(recv, recv, recv_sem).wait()

    total = jnp.zeros((8, columns), F32)
    for i in range(slots // chunk):
        got = recv[i * (chunk // CAP) : (i + 1) * (chunk // CAP)].reshape(chunk, WIDE)
        raw = jnp.dot(got, sky_wide[...], preferred_element_type=F32)
        peak = got[:, patches : patches + 1].astype(F32)
        limit = got[:, patches + 1 : patches + 2].astype(F32)
        rounded = jnp.minimum(raw * peak, limit).astype(BF16)
        power[i * chunk : (i + 1) * chunk, :] = rounded
        total = total + jnp.sum(rounded.astype(F32).reshape(chunk // 8, 8, columns), axis=0)
    flow = jnp.sum(total, axis=0, keepdims=True) * (1.0 / (4.0 * rows))
    for k in range(columns // 128):
        head[k : k + 1, :] = flow[:, 128 * k : 128 * (k + 1)]
    lanes = columns // 128
    head[lanes:, :] = jnp.full((8 - lanes, 128), station_ref[0], I32).astype(F32)
    own_head = pltpu.make_async_copy(head, heads.at[me], head_recv_sem)
    own_head.start()

    def tell(step, carry):
        pltpu.make_async_remote_copy(
            src_ref=head,
            dst_ref=heads.at[me],
            send_sem=head_send_sem,
            recv_sem=head_recv_sem,
            device_id=partner(step),
            device_id_type=MESH,
        ).start()
        return carry

    lax.fori_loop(1, feeders, tell, 0)

    live = live_ref[0].astype(F32)
    column = iota((8, WIDE), 1)
    weigh = jnp.where(column == patches + 2, 16.0, jnp.where(column == patches + 3, 1.0, 0.0)).astype(BF16)
    raw = nt_dot(weigh, recv[...].reshape(slots, WIDE))[0:1, :]
    node_row[...] = (raw - jnp.floor((raw + 0.5) / live) * live).astype(I32)
    node_block = 512
    for i in range(nodes // node_block):
        hit = jnp.where(iota((node_block, slots), 0) + node_block * i == node_row[...], 1.0, 0.0).astype(BF16)
        inject_ref[node_block * i : node_block * (i + 1), :] = jnp.dot(
            hit, power[...], preferred_element_type=F32
        ).astype(BF16)

    pltpu.make_async_copy(heads, heads, head_recv_sem).wait()
    stations = heads[:, lanes, :]
    picked = jnp.where(stations == iota((feeders, 128), 1).astype(F32), mv_ref[pl.ds(station_ref[0], 1), :], 0.0)
    weight = jnp.sum(picked, axis=1, keepdims=True)
    base_ref[...] = jnp.sum(heads[...] * weight[:, :, None], axis=0)

    def sent(step, carry):
        pltpu.make_async_copy(send.at[0], send.at[0], send_sem).wait()
        pltpu.make_async_copy(head, head, head_send_sem).wait()
        return carry

    lax.fori_loop(1, feeders, sent, 0)


def voltage_kernel(live_ref, matrix_ref, inject_ref, base_ref, out_ref):
    block, columns = out_ref.shape
    base = jnp.concatenate([base_ref[k : k + 1, :] for k in range(columns // 128)], axis=1)
    rise = jnp.dot(matrix_ref[...], inject_ref[...], preferred_element_type=F32)
    row = iota((block, columns), 0) + pl.program_id(0) * block
    out_ref[...] = jnp.where(row < live_ref[0], rise + base, 0.0).astype(BF16)


def on_device(
    regions,
    tiles,
    coefficients,
    peak_power,
    inverter_limit,
    building_feeder,
    building_node,
    sky_radiance,
    feeder_nodes,
    sensitivity,
    feeder_substation,
    mv_sensitivity,
):
    rows = coefficients.shape[0]
    nodes = sensitivity.shape[1]
    columns = sky_radiance.shape[1]
    feeders = regions * tiles
    slots = feeders * CAP
    vmem = pl.BlockSpec(memory_space=pltpu.VMEM)
    smem = pl.BlockSpec(memory_space=pltpu.SMEM)
    mv_wide = jnp.pad(mv_sensitivity, ((0, 0), (0, 128 - mv_sensitivity.shape[1])))
    inject, base = pl.pallas_call(
        functools.partial(exchange_kernel, regions, tiles),
        name="exchange",
        out_shape=(
            jax.ShapeDtypeStruct((nodes, columns), BF16),
            jax.ShapeDtypeStruct((8, 128), F32),
        ),
        in_specs=[vmem] * 6 + [smem] * 2 + [vmem],
        out_specs=(vmem, vmem),
        scratch_shapes=[
            pltpu.VMEM((WIDE, rows), BF16),
            pltpu.VMEM((WIDE, columns), BF16),
            pltpu.VMEM((feeders, CAP, WIDE), BF16),
            pltpu.VMEM((feeders, CAP, WIDE), BF16),
            pltpu.VMEM((slots, columns), BF16),
            pltpu.VMEM((1, slots), I32),
            pltpu.VMEM((8, 128), F32),
            pltpu.VMEM((feeders, 8, 128), F32),
            pltpu.SemaphoreType.DMA,
            pltpu.SemaphoreType.DMA,
            pltpu.SemaphoreType.DMA,
            pltpu.SemaphoreType.DMA,
        ],
        compiler_params=pltpu.CompilerParams(
            collective_id=0, has_side_effects=True, vmem_limit_bytes=48 * 1024 * 1024
        ),
    )(
        coefficients.T,
        building_feeder.reshape(1, rows),
        building_node.reshape(1, rows),
        peak_power.reshape(1, rows),
        inverter_limit.reshape(1, rows),
        sky_radiance,
        feeder_nodes,
        feeder_substation,
        mv_wide,
    )
    block = 512
    voltage = pl.pallas_call(
        voltage_kernel,
        name="voltage",
        grid=(nodes // block,),
        out_shape=jax.ShapeDtypeStruct((nodes, columns), BF16),
        in_specs=[
            smem,
            pl.BlockSpec((block, nodes), lambda i: (i, 0)),
            pl.BlockSpec((nodes, columns), lambda i: (0, 0)),
            pl.BlockSpec((8, 128), lambda i: (0, 0)),
        ],
        out_specs=pl.BlockSpec((block, columns), lambda i: (i, 0)),
        compiler_params=pltpu.CompilerParams(vmem_limit_bytes=40 * 1024 * 1024),
    )(feeder_nodes, sensitivity[0], inject, base)
    return voltage[None, :, :]


def solution(mesh):
    split = P(("region", "tile"))
    return jax.shard_map(
        functools.partial(on_device, mesh.shape["region"], mesh.shape["tile"]),
        mesh=mesh,
        in_specs=(
            P(("region", "tile"), None),
            split,
            split,
            P(("region", "tile"), None),
            split,
            P(),
            split,
            P(("region", "tile"), None, None),
            split,
            P(),
        ),
        out_specs=P(("region", "tile"), None, None),
        check_vma=False,
    )
```

time: 265 us -> 58.4 us (0.22)
  waiting for transfers between devices: 171 us -> 0 us
  Pallas kernels: 0 us -> 47.9 us
  other arithmetic: 28.3 us -> 0 us
  starting transfers between devices: 19.7 us -> 0 us
  between operations: 14.9 us -> 1.32 us
  matrix products: 13.5 us -> 0 us
  local copies, waits for them, and re-layouts: 17.3 us -> 8.75 us
    psum x1 -> x0, waiting for transfers between devices: 137 us -> none  [on_device(): totals = lax.psum(contribution, ('region', 'tile'))]
    pallas_call x0 -> x2, Pallas kernels: none -> 47.9 us  [the longest x1 39.7 us: on_device(): pl.pallas_call(functools.partial(exchange_kernel, regions, tiles), name='...]
    all_to_all x2 -> x0, waiting for transfers between devices: 33.5 us -> none  [the longest x1 31.7 us: move_rows(): lax.all_to_all(main_rows, ('region', 'tile'), split_axis=0, concat_axis=0...]
    all_to_all x2 -> x0, starting transfers between devices: 19.5 us -> none  [the longest x1 11.5 us: move_rows(): lax.all_to_all(node_buffer, ('region', 'tile'), split_axis=0, concat_axis...]
    scatter-add x1 -> x0, other arithmetic: 17.1 us -> none  [on_device(): inject = jnp.zeros((node_slots, columns), jnp.float32).at[local_node].add...]
    dot_general x3 -> x0, matrix products: 13.5 us -> none  [the longest x1 11.7 us: on_device(): jnp.dot(sensitivity[0], inject.astype(jnp.bfloat16), preferred_element_ty...]
    scatter x2 -> x0, local copies, waits for them, and re-layouts: 11.8 us -> none  [the longest x1 7.32 us: on_device(): jnp.zeros((slot_count, columns), jnp.bfloat16).at[position].set(pv_rows)]
    unnamed x12 -> x10, local copies, waits for them, and re-layouts: 0.02 us -> 6.66 us
  transfers between devices with their start and end apart: 3 -> 0, of which waited for: 3 -> 0; matrix products, arithmetic and copies ran while one was open for 6% -> 0% of each run, Pallas kernels for 0% -> 0%
where the time goes in v1:
time: 58.4 us; the launch traced here: 58 us
  Pallas kernels  47.9 us (82%)
  local copies, waits for them, and re-layouts  8.75 us (15%)
  between operations  1.32 us (2%)
    pallas_call x1, Pallas kernels, on_device(): pl.pallas_call(functools.partial(exchange_kernel, regions, tiles), name='...  39.7 us
    pallas_call x1, Pallas kernels, on_device(): pl.pallas_call(voltage_kernel, name='voltage', grid=(nodes // block,), ou...  8.19 us
    unnamed x10, local copies, waits for them, and re-layouts  6.66 us

profile of v1, /device:TPU:1, one launch (start us, length us, event | category | flops | bytes accessed | tf_op | source)
XLA Modules:
  0.0 58.0 jit_solution(1217397868753284420)
XLA Ops:
  1.3 0.7 %reshape.14.peak_ref = bf16[1,1024]{1,0:T(2,128)(2,1)S(1)} reshape(bf16[1024]{0:T(1024)(128)(2,1)} %param.11) | data formatting | bytes 4096 | tf_op jit(solution)/shard_map/reshape | solution.py:252
  2.0 0.7 %reshape.15.limit_ref = bf16[1,1024]{1,0:T(2,128)(2,1)S(1)} reshape(bf16[1024]{0:T(1024)(128)(2,1)} %param.12) | data formatting | bytes 4096 | tf_op jit(solution)/shard_map/reshape | solution.py:253
  2.7 0.7 %pad.4.mv_ref = f32[32,128]{1,0:T(8,128)S(1)} pad(f32[32,32]{1,0:T(8,128)} %param.19, f32[]{:T(128)} %constant.2.clone.1), padding=0_0x0_96 | pad | bytes 20484 | tf_op jit(solution)/shard_map/jit(_pad)/pad | solution.py:221
  3.4 0.0 copy-start.1
  3.4 1.0 %copy-done.1 = bf16[1024,145]{0,1:T(8,128)(2,1)S(1)} copy-done((bf16[1024,145]{0,1:T(8,128)(2,1)S(1)}, bf16[1024,145]{0,1:T(8,128)(2,1)}, u32[]{:S(2)}) %copy-start.1) | copy-done | bytes 296984
  4.4 0.0 copy-start.2
  4.4 0.9 %copy-done.2 = bf16[145,768]{1,0:T(8,128)(2,1)S(1)} copy-done((bf16[145,768]{1,0:T(8,128)(2,1)S(1)}, bf16[145,768]{1,0:T(8,128)(2,1)}, u32[]{:S(2)}) %copy-start.2) | copy-done | bytes 222744
  5.3 0.0 copy-start.3
  5.3 0.7 %copy-done.3 = s32[1024,1]{0,1:T(1,128)S(1)} copy-done((s32[1024,1]{0,1:T(1,128)S(1)}, s32[1024,1]{0,1:T(1,128)}, u32[]{:S(2)}) %copy-start.3) | copy-done | bytes 4120
  6.0 0.0 copy-start.4
  6.0 0.7 %copy-done.4 = s32[1024]{0:T(1024)S(1)} copy-done((s32[1024]{0:T(1024)S(1)}, s32[1024]{0:T(1024)}, u32[]{:S(2)}) %copy-start.4) | copy-done | bytes 4120
  6.7 39.7 %exchange.1 = (bf16[2048,768]{1,0:T(8,128)(2,1)S(1)}, f32[8,128]{1,0:T(8,128)S(1)}) custom-call(bf16[145,1024]{1,0:T(8,128)(2,1)S(1)} %bitcast.6, s32[1,1024]{1,0:T(1,128)S(1)} %bitcast.7, s32[1,1024]{1,0:T(1,128)S(1)} %bitcast.8, bf16[1,1024]{1,0:T(2,128)(2,1)S(1)} %reshape.14.peak_ref, bf16[1,1024]{1,0:T(2,128)(2,1)S(1)} %reshape.15.limit_ref, ...), custom_call_target="tpu_custom_call" | custom-call | tf_op jit(solution)/shard_map/exchange/pallas_call | solution.py:222
  46.4 0.0 copy-start
  46.4 3.4 %copy-done = bf16[1,2048,2048]{2,1,0:T(8,128)(2,1)S(1)} copy-done((bf16[1,2048,2048]{2,1,0:T(8,128)(2,1)S(1)}, bf16[1,2048,2048]{2,1,0:T(8,128)(2,1)}, u32[]{:S(2)}) %copy-start) | copy-done | bytes 8388632
  49.8 8.2 %voltage.1 = bf16[2048,768]{1,0:T(8,128)(2,1)} custom-call(s32[1]{0:T(128)S(6)} %copy.11.live_ref, bf16[2048,2048]{1,0:T(8,128)(2,1)S(1)} %bitcast.5, bf16[2048,768]{1,0:T(8,128)(2,1)S(1)} %get-tuple-element.7.inject_ref, f32[8,128]{1,0:T(8,128)S(1)} %get-tuple-element.8.base_ref), custom_call_target="tpu_custom_call" | custom-call | tf_op jit(solution)/shard_map/voltage/pallas_call | solution.py:260
Async XLA Ops:
  3.4 1.0 %copy-start.1 = (bf16[1024,145]{0,1:T(8,128)(2,1)S(1)}, bf16[1024,145]{0,1:T(8,128)(2,1)}, u32[]{:S(2)}) copy-start(bf16[1024,145]{0,1:T(8,128)(2,1)} %param.10) | copy-start | bytes 890884
  4.4 0.9 %copy-start.2 = (bf16[145,768]{1,0:T(8,128)(2,1)S(1)}, bf16[145,768]{1,0:T(8,128)(2,1)}, u32[]{:S(2)}) copy-start(bf16[145,768]{1,0:T(8,128)(2,1)} %sky_ref.1) | copy-start | bytes 668164
  5.3 0.7 %copy-start.3 = (s32[1024,1]{0,1:T(1,128)S(1)}, s32[1024,1]{0,1:T(1,128)}, u32[]{:S(2)}) copy-start(s32[1024,1]{0,1:T(1,128)} %param.13) | copy-start | bytes 12292
  6.0 0.7 %copy-start.4 = (s32[1024]{0:T(1024)S(1)}, s32[1024]{0:T(1024)}, u32[]{:S(2)}) copy-start(s32[1024]{0:T(1024)} %param.14) | copy-start | bytes 12292
  46.4 3.4 %copy-start = (bf16[1,2048,2048]{2,1,0:T(8,128)(2,1)S(1)}, bf16[1,2048,2048]{2,1,0:T(8,128)(2,1)}, u32[]{:S(2)}) copy-start(bf16[1,2048,2048]{2,1,0:T(8,128)(2,1)} %param.17) | copy-start | bytes 25165828
